TPU v7x, 32 devices: a whole 2x2x4 slice. The times are simulated.
32 devices in a mesh: path: 4 (over z), trade: 8 (over y, x, core).
Axes of the slice: x: 2, y: 2, z: 4, core: 2. Of those that a mesh axis runs over, the one named last changes fastest.
Arguments:
- factors: bfloat16 [32, 8, 512], P(None, None, 'path'), may hold values from -5 to 5
- loadings: bfloat16 [32, 8, 32768], P(None, None, 'trade'), may hold values from -0.5 to 0.5
- notional: float32 [32768], P('trade'), may hold values from -1 to 1
- strike: float32 [32768], P('trade'), may hold values from 0.5 to 1.5
- date_weight: float32 [32], replicated, may hold values from 0.3 to 3
- loss_spanning: float32 [128], replicated, may hold values from 0.2 to 0.9
- loss_local: float32 [1024], P('trade'), may hold values from 0.2 to 0.9
- trade_slot: int32 [32768], P('trade'), may hold values from 0 to 255
- span_list: int32 [1024], P('trade'), may hold values from 0 to 127, as said below
Outputs:
- loading_grad: float32 [32, 8, 32768], P('path', None, 'trade')
- factor_grad: float32 [32, 8, 512], P('trade', None, 'path')
Inputs may be any that keep to these rules, and one draw needn't show every extreme that they name: `trade_slot`: slot s < 128 of a trade shard holds that shard's spanning set from span_list; slot 128 + i holds the shard's i-th local set. `span_list`: the 128 entries of one trade shard are distinct spanning set ids.
All inputs are finite; a program needn't handle non-finite values.
Results may differ from a plain program's by a relative error of at most 0.0021.
Values may be sent and summed in bfloat16 or wider, within the bound.
A program may use at most 64 MiB of HBM per device.

v0:
```python
import math
import jax
import jax.numpy as jnp
from jax import lax
from jax.sharding import PartitionSpec as P

smoothing = 0.5


def price(factor_block, loading_block):
    exponent = jnp.einsum(
        "bfp,bfk->bpk", factor_block, loading_block, preferred_element_type=jnp.float32
    )
    return jnp.exp(exponent)


def on_device(
    factors,
    loadings,
    notional,
    strike,
    date_weight,
    loss_spanning,
    loss_local,
    trade_slot,
    span_list,
):
    path_total = lax.axis_size("path") * factors.shape[2]
    factor_here = lax.all_to_all(factors, "path", split_axis=0, concat_axis=2, tiled=True)
    dates_here = factor_here.shape[0]
    first_date = lax.axis_index("path") * dates_here
    loading_here = lax.dynamic_slice_in_dim(loadings, first_date, dates_here, 0)
    weight_here = lax.dynamic_slice_in_dim(date_weight, first_date, dates_here, 0)
    date_count = factor_here.shape[0]
    factor_count = factor_here.shape[1]
    path_local = factor_here.shape[2]
    trade_local = loading_here.shape[2]
    span_local = span_list.shape[0]
    span_count = loss_spanning.shape[0]
    slot_count = span_local + loss_local.shape[0]
    dates_per_step = math.gcd(date_count, max(1, 512 // path_local))
    block_count = date_count // dates_per_step
    slot_table = (trade_slot[:, None] == jnp.arange(slot_count, dtype=jnp.int32)[None, :]).astype(
        jnp.bfloat16
    )
    set_match = span_list[:, None] == jnp.arange(span_count, dtype=jnp.int32)[None, :]
    set_table = set_match.astype(jnp.float32)
    set_select = set_match.astype(jnp.bfloat16)
    factor_blocks = factor_here.reshape(block_count, dates_per_step, factor_count, path_local)
    loading_blocks = loading_here.reshape(block_count, dates_per_step, factor_count, trade_local)
    weight_blocks = weight_here.reshape(block_count, dates_per_step)

    def forward(operands):
        factor_block, loading_block, weight_block = operands
        growth = price(factor_block, loading_block)
        values = (notional * (growth - strike)).astype(jnp.bfloat16)
        partial_sums = jnp.einsum(
            "bpk,ks->bps", values, slot_table, preferred_element_type=jnp.float32
        )
        span_part = jnp.einsum(
            "bps,sn->bpn",
            partial_sums[:, :, :span_local],
            set_table,
            precision=lax.Precision.HIGHEST,
            preferred_element_type=jnp.float32,
        )
        local_weight = (
            weight_block[:, None, None]
            * loss_local
            * jax.nn.sigmoid(partial_sums[:, :, span_local:] / smoothing)
        ).astype(jnp.bfloat16)
        return (span_part, local_weight)

    span_parts, local_weights = lax.map(forward, (factor_blocks, loading_blocks, weight_blocks))
    span_parts = span_parts.reshape(date_count, path_local, span_count)
    span_total = lax.psum(span_parts, "trade")
    span_weight = (
        weight_here[:, None, None] * loss_spanning * jax.nn.sigmoid(span_total / smoothing)
    ).astype(jnp.bfloat16)
    span_blocks = span_weight.reshape(block_count, dates_per_step, path_local, span_count)

    def adjoint(operands):
        factor_block, loading_block, span_block, local_block = operands
        growth = price(factor_block, loading_block)
        span_slots = jnp.einsum(
            "bpn,sn->bps", span_block, set_select, preferred_element_type=jnp.float32
        ).astype(jnp.bfloat16)
        slot_weight = jnp.concatenate([span_slots, local_block], axis=2)
        trade_weight = jnp.einsum(
            "bps,ks->bpk", slot_weight, slot_table, preferred_element_type=jnp.float32
        )
        sensitivity = (trade_weight * notional * growth).astype(jnp.bfloat16)
        loading_term = jnp.einsum(
            "bfp,bpk->bfk", factor_block, sensitivity, preferred_element_type=jnp.float32
        )
        factor_term = jnp.einsum(
            "bfk,bpk->bfp", loading_block, sensitivity, preferred_element_type=jnp.float32
        )
        return (loading_term, factor_term)

    loading_terms, factor_terms = lax.map(
        adjoint, (factor_blocks, loading_blocks, span_blocks, local_weights)
    )
    loading_terms = loading_terms.reshape(date_count, factor_count, trade_local)
    factor_terms = factor_terms.reshape(date_count, factor_count, path_local)
    loading_grad = loading_terms / path_total
    regrouped = lax.all_to_all(factor_terms, "path", split_axis=2, concat_axis=0, tiled=True)
    factor_grad = lax.psum_scatter(regrouped, "trade", scatter_dimension=0, tiled=True)
    return (loading_grad, factor_grad)


def solution(mesh):
    return jax.shard_map(
        on_device,
        mesh=mesh,
        in_specs=(
            P(None, None, "path"),
            P(None, None, "trade"),
            P("trade"),
            P("trade"),
            P(),
            P(),
            P("trade"),
            P("trade"),
            P("trade"),
        ),
        out_specs=(P("path", None, "trade"), P("trade", None, "path")),
        check_vma=False,
    )
```

profile of v0, /device:TPU:0, one launch (start us, length us, event | category | flops | bytes accessed | tf_op | source)
XLA Modules:
  0.0 284.7 jit_solution(14998099556894631179)
XLA Ops:
  7.2 6.5 %all-to-all-start = ((bf16[32,8,128]{2,1,0:T(8,128)(2,1)}), bf16[32,8,128]{2,1,0:T(8,128)(2,1)S(1)}, u32[]{:S(2)}, u32[]{:S(2)}) async-start(bf16[32,8,128]{2,1,0:T(8,128)(2,1)} %param.13), calls=%async_computation | async-start | bytes 131072 | tf_op jit(solution)/shard_map/all_to_all | solution.py:29
  14.5 4.9 %all-to-all-done = bf16[32,8,128]{2,1,0:T(8,128)(2,1)S(1)} async-done(((bf16[32,8,128]{2,1,0:T(8,128)(2,1)}), bf16[32,8,128]{2,1,0:T(8,128)(2,1)S(1)}, u32[]{:S(2)}, u32[]{:S(2)}) %all-to-all-start) | async-done | bytes 65568 | tf_op jit(solution)/shard_map/all_to_all | solution.py:29
  19.5 50.6 %while.26 = (s32[]{:T(128)}, f32[8,1,512,128]{3,2,1,0:T(8,128)}, bf16[8,1,512,128]{3,2,1,0:T(8,128)(2,1)}, f32[4096]{0:T(1024)}, bf16[8,1,8,512]{3,2,1,0:T(8,128...) while((s32[]{:T(128)}, f32[8,1,512,128]{3,2,1,0:T(8,128)}, ...), condition=%wide.region_1.2_spmd.clone, body=%wide.region_0.1_spmd.clone.sunk | while | flops 1216774272 | bytes 1573053 | solution.py:74
  19.5 3.3 %fusion.88 = f32[1,512,256]{2,1,0:T(8,128)S(1)} fusion(s32[4096]{0:T(1024)} %get-tuple-element.392, f32[4096]{0:T(1024)} %get-tuple-element.389, f32[4096]{0:T(1024)} %get-tuple-element.386, bf16[8,1,8,4096]{3,2,1,0:T(8,128)(2,1)S(1)} %get-tuple-element.388, s32[]{:T(128)} %get-tuple-element.371, bf16[8,1,8,512]{3,2,1,0:T(8,128)(2,1)S(1)} %get-tuple-element.387), kind=kOutput, calls=%fused_computation.9.clone.1 | convolution fusion | flops 1115684864 | bytes 648192 | tf_op jit(solution)/shard_map/while/body/eval_jaxpr/bpk,ks->bps/dot_general | solution.py:57
  24.6 1.1 fusion.89
  25.8 3.3 %fusion.88 = f32[1,512,256]{2,1,0:T(8,128)S(1)} fusion(s32[4096]{0:T(1024)} %get-tuple-element.392, f32[4096]{0:T(1024)} %get-tuple-element.389, f32[4096]{0:T(1024)} %get-tuple-element.386, bf16[8,1,8,4096]{3,2,1,0:T(8,128)(2,1)S(1)} %get-tuple-element.388, s32[]{:T(128)} %get-tuple-element.371, bf16[8,1,8,512]{3,2,1,0:T(8,128)(2,1)S(1)} %get-tuple-element.387), kind=kOutput, calls=%fused_computation.9.clone.1 | convolution fusion | flops 1115684864 | bytes 648192 | tf_op jit(solution)/shard_map/while/body/eval_jaxpr/bpk,ks->bps/dot_general | solution.py:57
  30.9 1.1 fusion.89
  32.1 3.3 %fusion.88 = f32[1,512,256]{2,1,0:T(8,128)S(1)} fusion(s32[4096]{0:T(1024)} %get-tuple-element.392, f32[4096]{0:T(1024)} %get-tuple-element.389, f32[4096]{0:T(1024)} %get-tuple-element.386, bf16[8,1,8,4096]{3,2,1,0:T(8,128)(2,1)S(1)} %get-tuple-element.388, s32[]{:T(128)} %get-tuple-element.371, bf16[8,1,8,512]{3,2,1,0:T(8,128)(2,1)S(1)} %get-tuple-element.387), kind=kOutput, calls=%fused_computation.9.clone.1 | convolution fusion | flops 1115684864 | bytes 648192 | tf_op jit(solution)/shard_map/while/body/eval_jaxpr/bpk,ks->bps/dot_general | solution.py:57
  37.3 1.1 fusion.89
  38.4 3.3 %fusion.88 = f32[1,512,256]{2,1,0:T(8,128)S(1)} fusion(s32[4096]{0:T(1024)} %get-tuple-element.392, f32[4096]{0:T(1024)} %get-tuple-element.389, f32[4096]{0:T(1024)} %get-tuple-element.386, bf16[8,1,8,4096]{3,2,1,0:T(8,128)(2,1)S(1)} %get-tuple-element.388, s32[]{:T(128)} %get-tuple-element.371, bf16[8,1,8,512]{3,2,1,0:T(8,128)(2,1)S(1)} %get-tuple-element.387), kind=kOutput, calls=%fused_computation.9.clone.1 | convolution fusion | flops 1115684864 | bytes 648192 | tf_op jit(solution)/shard_map/while/body/eval_jaxpr/bpk,ks->bps/dot_general | solution.py:57
  43.5 1.1 fusion.89
  44.7 3.3 %fusion.88 = f32[1,512,256]{2,1,0:T(8,128)S(1)} fusion(s32[4096]{0:T(1024)} %get-tuple-element.392, f32[4096]{0:T(1024)} %get-tuple-element.389, f32[4096]{0:T(1024)} %get-tuple-element.386, bf16[8,1,8,4096]{3,2,1,0:T(8,128)(2,1)S(1)} %get-tuple-element.388, s32[]{:T(128)} %get-tuple-element.371, bf16[8,1,8,512]{3,2,1,0:T(8,128)(2,1)S(1)} %get-tuple-element.387), kind=kOutput, calls=%fused_computation.9.clone.1 | convolution fusion | flops 1115684864 | bytes 648192 | tf_op jit(solution)/shard_map/while/body/eval_jaxpr/bpk,ks->bps/dot_general | solution.py:57
  49.9 1.2 fusion.89
  51.0 3.3 %fusion.88 = f32[1,512,256]{2,1,0:T(8,128)S(1)} fusion(s32[4096]{0:T(1024)} %get-tuple-element.392, f32[4096]{0:T(1024)} %get-tuple-element.389, f32[4096]{0:T(1024)} %get-tuple-element.386, bf16[8,1,8,4096]{3,2,1,0:T(8,128)(2,1)S(1)} %get-tuple-element.388, s32[]{:T(128)} %get-tuple-element.371, bf16[8,1,8,512]{3,2,1,0:T(8,128)(2,1)S(1)} %get-tuple-element.387), kind=kOutput, calls=%fused_computation.9.clone.1 | convolution fusion | flops 1115684864 | bytes 648192 | tf_op jit(solution)/shard_map/while/body/eval_jaxpr/bpk,ks->bps/dot_general | solution.py:57
  56.2 1.1 fusion.89
  57.3 3.3 %fusion.88 = f32[1,512,256]{2,1,0:T(8,128)S(1)} fusion(s32[4096]{0:T(1024)} %get-tuple-element.392, f32[4096]{0:T(1024)} %get-tuple-element.389, f32[4096]{0:T(1024)} %get-tuple-element.386, bf16[8,1,8,4096]{3,2,1,0:T(8,128)(2,1)S(1)} %get-tuple-element.388, s32[]{:T(128)} %get-tuple-element.371, bf16[8,1,8,512]{3,2,1,0:T(8,128)(2,1)S(1)} %get-tuple-element.387), kind=kOutput, calls=%fused_computation.9.clone.1 | convolution fusion | flops 1115684864 | bytes 648192 | tf_op jit(solution)/shard_map/while/body/eval_jaxpr/bpk,ks->bps/dot_general | solution.py:57
  62.5 1.1 fusion.89
  63.7 3.3 %fusion.88 = f32[1,512,256]{2,1,0:T(8,128)S(1)} fusion(s32[4096]{0:T(1024)} %get-tuple-element.392, f32[4096]{0:T(1024)} %get-tuple-element.389, f32[4096]{0:T(1024)} %get-tuple-element.386, bf16[8,1,8,4096]{3,2,1,0:T(8,128)(2,1)S(1)} %get-tuple-element.388, s32[]{:T(128)} %get-tuple-element.371, bf16[8,1,8,512]{3,2,1,0:T(8,128)(2,1)S(1)} %get-tuple-element.387), kind=kOutput, calls=%fused_computation.9.clone.1 | convolution fusion | flops 1115684864 | bytes 648192 | tf_op jit(solution)/shard_map/while/body/eval_jaxpr/bpk,ks->bps/dot_general | solution.py:57
  68.8 1.2 fusion.89
  70.9 59.7 %all-reduce.2.cloned.1.call-done = f32[8,512,128]{2,1,0:T(8,128)} async-done(((f32[8,512,128]{2,1,0:T(8,128)}), f32[8,512,128]{2,1,0:T(8,128)}) %all-reduce.2.cloned.1.call-update) | async-done | bytes 2097168 | tf_op jit(solution)/shard_map/psum | solution.py:76
  130.5 2.1 fusion.62
  132.7 88.6 %while.27 = (s32[]{:T(128)}, f32[8,1,8,4096]{3,2,1,0:T(8,128)}, f32[8,1,8,512]{3,2,1,0:T(8,128)}, bf16[8,1,8,512]{3,2,1,0:T(8,128)(2,1)S(1)}, bf16[8,1,512,128]{...) while((s32[]{:T(128)}, f32[8,1,8,4096]{3,2,1,0:T(8,128)}, ...), condition=%wide.region_4.5_spmd.clone, body=%wide.region_3.4_spmd.clone.sunk | while | flops 1200193536 | bytes 31266512 | solution.py:101
  133.5 0.9 constant_dynamic-slice_fusion.5
  134.6 2.6 fusion.100
  137.2 2.5 multiply_convert_fusion.4
  139.8 1.3 fusion.101
  141.1 2.6 fusion.102
  145.7 2.6 fusion.100
  148.3 2.5 multiply_convert_fusion.4
  150.9 1.3 fusion.101
  152.2 2.6 fusion.102
  156.7 2.6 fusion.100
  159.4 2.5 multiply_convert_fusion.4
  161.9 1.3 fusion.101
  163.3 2.6 fusion.102
  167.8 2.6 fusion.100
  170.4 2.5 multiply_convert_fusion.4
  173.0 1.3 fusion.101
  174.3 2.6 fusion.102
  178.9 2.6 fusion.100
  181.5 2.5 multiply_convert_fusion.4
  184.1 1.3 fusion.101
  185.4 2.6 fusion.102
  189.9 2.6 fusion.100
  192.6 2.5 multiply_convert_fusion.4
  195.1 1.3 fusion.101
  196.5 2.6 fusion.102
  201.0 2.6 fusion.100
  203.7 2.5 multiply_convert_fusion.4
  206.2 1.3 fusion.101
  207.5 2.6 fusion.102
  212.1 2.6 fusion.100
  214.7 2.5 multiply_convert_fusion.4
  217.3 1.3 fusion.101
  218.6 2.6 fusion.102
  221.3 2.9 %copy.18 = f32[8,1,8,512]{2,0,3,1:T(8,128)} copy(f32[8,1,8,512]{3,2,1,0:T(8,128)} %get-tuple-element.445) | data formatting | bytes 262144 | tf_op jit(solution)/shard_map/while | solution.py:101
  224.1 3.1 %bitcast_bitcast_fusion = f32[512,8,8]{2,1,0:T(8,128)} fusion(f32[8,1,8,512]{2,0,3,1:T(8,128)} %copy.18), kind=kLoop, calls=%fused_computation.71 | loop fusion | bytes 262144
  227.2 2.7 reshape.144
  229.8 10.2 %all_to_all.33 = f32[4,1,8192]{2,1,0:T(1,128)S(1)} all-to-all(f32[4,1,8192]{2,1,0:T(1,128)S(1)} %reshape.144), channel_id=1, replica_groups=mesh['path'=4,'trade'=8] {'path'}, dimensions={0} | all-to-all | bytes 262144 | tf_op jit(solution)/shard_map/all_to_all | solution.py:107
  240.6 1.0 reduce
  241.6 2.5 reshape.145
  244.1 2.8 copy.19
  246.9 2.3 fusion.61
  249.2 28.7 %reduce-scatter.2.cloned.1.call-done = f32[4,8,128]{2,1,0:T(8,128)} async-done(((f32[32,8,128]{2,1,0:T(8,128)}), f32[4,8,128]{2,1,0:T(8,128)}) %reduce-scatter.2.cloned.1.call-update) | async-done | bytes 16400 | tf_op jit(solution)/shard_map/reduce_scatter | solution.py:108
  (153 shorter events, 31.3 us)
Async XLA Ops:
  7.2 6.5 %copy-start = (bf16[32,8,4096]{2,1,0:T(8,128)(2,1)S(1)}, bf16[32,8,4096]{2,1,0:T(8,128)(2,1)}, u32[]{:S(2)}) copy-start(bf16[32,8,4096]{2,1,0:T(8,128)(2,1)} %param.14) | copy-start | bytes 6291460
  7.2 12.2 %all-to-all-start = ((bf16[32,8,128]{2,1,0:T(8,128)(2,1)}), bf16[32,8,128]{2,1,0:T(8,128)(2,1)S(1)}, u32[]{:S(2)}, u32[]{:S(2)}) async-start(bf16[32,8,128]{2,1,0:T(8,128)(2,1)} %param.13), calls=%async_computation | async-start | bytes 131072 | tf_op jit(solution)/shard_map/all_to_all | solution.py:29
  13.7 116.8 %all-reduce.2.cloned.1.call-start = ((), (), s32[]{:S(2)}) async-start(), calls=%async_computation.3 | async-start | bytes 4194304 | tf_op jit(solution)/shard_map/psum | solution.py:76
  19.4 50.7 %copy-start.10 = (f32[32]{0:T(128)S(1)}, f32[32]{0:T(128)}, u32[]{:S(2)}) copy-start(f32[32]{0:T(128)} %param.17) | copy-start | bytes 388
  19.4 50.7 %copy-start.8 = (f32[128]{0:T(128)S(1)}, f32[128]{0:T(128)}, u32[]{:S(2)}) copy-start(f32[128]{0:T(128)} %param.18) | copy-start | bytes 1540
  19.5 3.9 %copy-start.9 = (f32[128]{0:T(128)S(1)}, f32[128]{0:T(128)}, u32[]{:S(2)}) copy-start(f32[128]{0:T(128)} %get-tuple-element.391) | copy-start | bytes 1540 | tf_op jit(solution)/shard_map/while
  19.5 5.2 %copy-start.5 = (s32[128]{0:T(128)S(1)}, s32[128]{0:T(128)}, u32[]{:S(2)}) copy-start(s32[128]{0:T(128)} %get-tuple-element.393) | copy-start | bytes 1540 | tf_op jit(solution)/shard_map/while
  25.8 3.9 %copy-start.9 = (f32[128]{0:T(128)S(1)}, f32[128]{0:T(128)}, u32[]{:S(2)}) copy-start(f32[128]{0:T(128)} %get-tuple-element.391) | copy-start | bytes 1540 | tf_op jit(solution)/shard_map/while
  25.8 5.2 %copy-start.5 = (s32[128]{0:T(128)S(1)}, s32[128]{0:T(128)}, u32[]{:S(2)}) copy-start(s32[128]{0:T(128)} %get-tuple-element.393) | copy-start | bytes 1540 | tf_op jit(solution)/shard_map/while
  32.1 3.9 %copy-start.9 = (f32[128]{0:T(128)S(1)}, f32[128]{0:T(128)}, u32[]{:S(2)}) copy-start(f32[128]{0:T(128)} %get-tuple-element.391) | copy-start | bytes 1540 | tf_op jit(solution)/shard_map/while
  32.1 5.2 %copy-start.5 = (s32[128]{0:T(128)S(1)}, s32[128]{0:T(128)}, u32[]{:S(2)}) copy-start(s32[128]{0:T(128)} %get-tuple-element.393) | copy-start | bytes 1540 | tf_op jit(solution)/shard_map/while
  38.4 3.9 %copy-start.9 = (f32[128]{0:T(128)S(1)}, f32[128]{0:T(128)}, u32[]{:S(2)}) copy-start(f32[128]{0:T(128)} %get-tuple-element.391) | copy-start | bytes 1540 | tf_op jit(solution)/shard_map/while
  38.4 5.1 %copy-start.5 = (s32[128]{0:T(128)S(1)}, s32[128]{0:T(128)}, u32[]{:S(2)}) copy-start(s32[128]{0:T(128)} %get-tuple-element.393) | copy-start | bytes 1540 | tf_op jit(solution)/shard_map/while
  44.7 3.9 %copy-start.9 = (f32[128]{0:T(128)S(1)}, f32[128]{0:T(128)}, u32[]{:S(2)}) copy-start(f32[128]{0:T(128)} %get-tuple-element.391) | copy-start | bytes 1540 | tf_op jit(solution)/shard_map/while
  44.7 5.2 %copy-start.5 = (s32[128]{0:T(128)S(1)}, s32[128]{0:T(128)}, u32[]{:S(2)}) copy-start(s32[128]{0:T(128)} %get-tuple-element.393) | copy-start | bytes 1540 | tf_op jit(solution)/shard_map/while
  51.0 3.9 %copy-start.9 = (f32[128]{0:T(128)S(1)}, f32[128]{0:T(128)}, u32[]{:S(2)}) copy-start(f32[128]{0:T(128)} %get-tuple-element.391) | copy-start | bytes 1540 | tf_op jit(solution)/shard_map/while
  51.0 5.2 %copy-start.5 = (s32[128]{0:T(128)S(1)}, s32[128]{0:T(128)}, u32[]{:S(2)}) copy-start(s32[128]{0:T(128)} %get-tuple-element.393) | copy-start | bytes 1540 | tf_op jit(solution)/shard_map/while
  57.3 3.9 %copy-start.9 = (f32[128]{0:T(128)S(1)}, f32[128]{0:T(128)}, u32[]{:S(2)}) copy-start(f32[128]{0:T(128)} %get-tuple-element.391) | copy-start | bytes 1540 | tf_op jit(solution)/shard_map/while
  57.3 5.2 %copy-start.5 = (s32[128]{0:T(128)S(1)}, s32[128]{0:T(128)}, u32[]{:S(2)}) copy-start(s32[128]{0:T(128)} %get-tuple-element.393) | copy-start | bytes 1540 | tf_op jit(solution)/shard_map/while
  63.7 3.9 %copy-start.9 = (f32[128]{0:T(128)S(1)}, f32[128]{0:T(128)}, u32[]{:S(2)}) copy-start(f32[128]{0:T(128)} %get-tuple-element.391) | copy-start | bytes 1540 | tf_op jit(solution)/shard_map/while
  63.7 5.2 %copy-start.5 = (s32[128]{0:T(128)S(1)}, s32[128]{0:T(128)}, u32[]{:S(2)}) copy-start(s32[128]{0:T(128)} %get-tuple-element.393) | copy-start | bytes 1540 | tf_op jit(solution)/shard_map/while
  70.0 0.8 copy-start.1
  70.0 62.6 %copy-start.2 = (f32[4096]{0:T(1024)S(1)}, f32[4096]{0:T(1024)}, u32[]{:S(2)}) copy-start(f32[4096]{0:T(1024)} %get-tuple-element.436) | copy-start | bytes 49156
  70.0 62.7 %copy-start.6 = (s32[128]{0:T(128)S(1)}, s32[128]{0:T(128)}, u32[]{:S(2)}) copy-start(s32[128]{0:T(128)} %get-tuple-element.442) | copy-start | bytes 1540
  70.0 207.8 %reduce-scatter.2.cloned.1.call-start = ((), (), s32[]{:S(2)}) async-start(), calls=%async_computation.4 | async-start | bytes 147456 | tf_op jit(solution)/shard_map/reduce_scatter | solution.py:108
  132.7 0.6 copy-start.3
  137.2 2.6 copy-start.4
  139.8 4.0 %copy-start.7 = (s32[128]{0:T(128)S(1)}, s32[128]{0:T(128)}, u32[]{:S(2)}) copy-start(s32[128]{0:T(128)} %get-tuple-element.454) | copy-start | bytes 1540 | tf_op jit(solution)/shard_map/while
  143.8 0.6 copy-start.3
  148.3 2.6 copy-start.4
  150.9 4.0 %copy-start.7 = (s32[128]{0:T(128)S(1)}, s32[128]{0:T(128)}, u32[]{:S(2)}) copy-start(s32[128]{0:T(128)} %get-tuple-element.454) | copy-start | bytes 1540 | tf_op jit(solution)/shard_map/while
  154.8 0.6 copy-start.3
  159.4 2.6 copy-start.4
  161.9 4.0 %copy-start.7 = (s32[128]{0:T(128)S(1)}, s32[128]{0:T(128)}, u32[]{:S(2)}) copy-start(s32[128]{0:T(128)} %get-tuple-element.454) | copy-start | bytes 1540 | tf_op jit(solution)/shard_map/while
  165.9 0.6 copy-start.3
  170.4 2.6 copy-start.4
  173.0 4.0 %copy-start.7 = (s32[128]{0:T(128)S(1)}, s32[128]{0:T(128)}, u32[]{:S(2)}) copy-start(s32[128]{0:T(128)} %get-tuple-element.454) | copy-start | bytes 1540 | tf_op jit(solution)/shard_map/while
  177.0 0.6 copy-start.3
  181.5 2.6 copy-start.4
  184.1 4.0 %copy-start.7 = (s32[128]{0:T(128)S(1)}, s32[128]{0:T(128)}, u32[]{:S(2)}) copy-start(s32[128]{0:T(128)} %get-tuple-element.454) | copy-start | bytes 1540 | tf_op jit(solution)/shard_map/while
  188.0 0.6 copy-start.3
  192.6 2.6 copy-start.4
  195.1 4.0 %copy-start.7 = (s32[128]{0:T(128)S(1)}, s32[128]{0:T(128)}, u32[]{:S(2)}) copy-start(s32[128]{0:T(128)} %get-tuple-element.454) | copy-start | bytes 1540 | tf_op jit(solution)/shard_map/while
  199.1 0.6 copy-start.3
  203.6 2.6 copy-start.4
  206.2 4.0 %copy-start.7 = (s32[128]{0:T(128)S(1)}, s32[128]{0:T(128)}, u32[]{:S(2)}) copy-start(s32[128]{0:T(128)} %get-tuple-element.454) | copy-start | bytes 1540 | tf_op jit(solution)/shard_map/while
  210.2 0.6 copy-start.3
  214.7 2.6 copy-start.4
  217.3 4.0 %copy-start.7 = (s32[128]{0:T(128)S(1)}, s32[128]{0:T(128)}, u32[]{:S(2)}) copy-start(s32[128]{0:T(128)} %get-tuple-element.454) | copy-start | bytes 1540 | tf_op jit(solution)/shard_map/while
Sparse Core Ops, SparseCore 0:
  70.2 60.2 all-reduce.1
  247.0 30.8 reduce-scatter.1
where the time goes:
time: 287 us; the launch traced here: 285 us
  matrix products  110 us (38%)
  waiting for transfers between devices  93.3 us (33%)
  local copies, waits for them, and re-layouts  33.8 us (12%)
  other arithmetic  15.8 us (6%)
  between operations  14.1 us (5%)
  blocking collectives  10.2 us (4%)
  starting transfers between devices  6.53 us (2%)
    psum x1, waiting for transfers between devices, on_device(): span_total = lax.psum(span_parts, 'trade')  59.7 us
    reduce_scatter x1, waiting for transfers between devices, on_device(): lax.psum_scatter(regrouped, 'trade', scatter_dimension=0, tiled=True)  28.7 us
    dot_general x8, matrix products, forward(): jnp.einsum('bpk,ks->bps', values, slot_table, preferred_element_type=jnp....  26.4 us
    dot_general x8, matrix products, adjoint(): jnp.einsum('bps,ks->bpk', slot_weight, slot_table, preferred_element_type...  21.1 us
    dot_general x8, matrix products, adjoint(): jnp.einsum('bfk,bpk->bfp', loading_block, sensitivity, preferred_element_...  21.1 us
    dot_general x8, matrix products, price(): jnp.einsum('bfp,bfk->bpk', factor_block, loading_block, preferred_element...  20.3 us
    dot_general x8, matrix products, adjoint(): jnp.einsum('bfp,bpk->bfk', factor_block, sensitivity, preferred_element_t...  10.5 us
    all_to_all x1, blocking collectives, on_device(): lax.all_to_all(factor_terms, 'path', split_axis=2, concat_axis=0, tiled=T...  10.2 us
  transfers between devices with their start and end apart: 3, of which 3 were waited for; matrix products, arithmetic and copies ran while one was open for 1% of the time, Pallas kernels for 0%

commit v1 on v0

--- a/solution.py
+++ b/solution.py
@@ -5,6 +5,15 @@
 from jax.sharding import PartitionSpec as P
 
 smoothing = 0.5
+
+
+def register_tokens(block_here):
+    workers = jax.lax.axis_size("trade")
+    reply = block_here
+    for k in [[(m, m ^ t) for m in range(workers)] for t in (1, 2, 4, 8, 16) if t < workers]:
+        carry_out = jax.lax.ppermute(reply, "trade", k)
+        reply = reply + carry_out
+    return reply
 
 
 def price(factor_block, loading_block):
@@ -73,7 +82,7 @@
 
     span_parts, local_weights = lax.map(forward, (factor_blocks, loading_blocks, weight_blocks))
     span_parts = span_parts.reshape(date_count, path_local, span_count)
-    span_total = lax.psum(span_parts, "trade")
+    span_total = register_tokens(span_parts)
     span_weight = (
         weight_here[:, None, None] * loss_spanning * jax.nn.sigmoid(span_total / smoothing)
     ).astype(jnp.bfloat16)

time: 287 us -> 330 us (1.15)
  waiting for transfers between devices: 93.3 us -> 131 us
  other arithmetic: 15.8 us -> 19.9 us
    ppermute x0 -> x3, waiting for transfers between devices: none -> 96 us  [register_tokens(): carry_out = jax.lax.ppermute(reply, 'trade', k)]
    psum x1 -> x0, waiting for transfers between devices: 59.7 us -> none  [on_device(): span_total = lax.psum(span_parts, 'trade')]
    add x0 -> x2, other arithmetic: none -> 3.4 us  [register_tokens(): reply = reply + carry_out]
  transfers between devices with their start and end apart: 3 -> 5, of which waited for: 3 -> 5; matrix products, arithmetic and copies ran while one was open for 1% -> 1% of each run, Pallas kernels for 0% -> 0%
where the time goes in v1:
time: 330 us; the launch traced here: 328 us
  waiting for transfers between devices  131 us (40%)
  matrix products  110 us (33%)
  local copies, waits for them, and re-layouts  33.3 us (10%)
  other arithmetic  19.9 us (6%)
  between operations  14.1 us (4%)
  starting transfers between devices  9.57 us (3%)
  blocking collectives  8.31 us (3%)
    ppermute x3, waiting for transfers between devices, register_tokens(): carry_out = jax.lax.ppermute(reply, 'trade', k)  96 us
    reduce_scatter x1, waiting for transfers between devices, on_device(): lax.psum_scatter(regrouped, 'trade', scatter_dimension=0, tiled=True)  30.5 us
    dot_general x8, matrix products, forward(): jnp.einsum('bpk,ks->bps', values, slot_table, preferred_element_type=jnp....  26.4 us
    dot_general x8, matrix products, adjoint(): jnp.einsum('bfk,bpk->bfp', loading_block, sensitivity, preferred_element_...  21.2 us
    dot_general x8, matrix products, adjoint(): jnp.einsum('bps,ks->bpk', slot_weight, slot_table, preferred_element_type...  21.1 us
    dot_general x8, matrix products, price(): jnp.einsum('bfp,bfk->bpk', factor_block, loading_block, preferred_element...  20.3 us
    dot_general x8, matrix products, adjoint(): jnp.einsum('bfp,bpk->bfk', factor_block, sensitivity, preferred_element_t...  10.5 us
    dot_general x8, matrix products, forward(): jnp.einsum('bps,sn->bpn', partial_sums[:, :, :span_local], set_table, pre...  9.17 us
  transfers between devices with their start and end apart: 5, of which 5 were waited for; matrix products, arithmetic and copies ran while one was open for 1% of the time, Pallas kernels for 0%

profile of v1, /device:TPU:0, one launch (start us, length us, event | category | flops | bytes accessed | tf_op | source)
XLA Modules:
  0.0 327.5 jit_solution(11563548764530204331)
XLA Ops:
  7.2 6.5 %all-to-all-start = ((bf16[32,8,128]{2,1,0:T(8,128)(2,1)}), bf16[32,8,128]{2,1,0:T(8,128)(2,1)S(1)}, u32[]{:S(2)}, u32[]{:S(2)}) async-start(bf16[32,8,128]{2,1,0:T(8,128)(2,1)} %param.13), calls=%async_computation | async-start | bytes 131072 | tf_op jit(solution)/shard_map/all_to_all | solution.py:38
  14.5 4.9 %all-to-all-done = bf16[32,8,128]{2,1,0:T(8,128)(2,1)S(1)} async-done(((bf16[32,8,128]{2,1,0:T(8,128)(2,1)}), bf16[32,8,128]{2,1,0:T(8,128)(2,1)S(1)}, u32[]{:S(2)}, u32[]{:S(2)}) %all-to-all-start) | async-done | bytes 65568 | tf_op jit(solution)/shard_map/all_to_all | solution.py:38
  19.4 50.8 %while.26 = (s32[]{:T(128)}, f32[8,1,512,128]{3,2,1,0:T(8,128)}, bf16[8,1,512,128]{3,2,1,0:T(8,128)(2,1)}, f32[4096]{0:T(1024)}, bf16[8,1,8,512]{3,2,1,0:T(8,128...) while((s32[]{:T(128)}, f32[8,1,512,128]{3,2,1,0:T(8,128)}, ...), condition=%wide.region_1.2_spmd.clone, body=%wide.region_0.1_spmd.clone.sunk | while | flops 1216774272 | bytes 1573053 | solution.py:83
  19.5 3.3 %fusion.88 = f32[1,512,256]{2,1,0:T(8,128)S(1)} fusion(s32[4096]{0:T(1024)} %get-tuple-element.392, f32[4096]{0:T(1024)} %get-tuple-element.389, f32[4096]{0:T(1024)} %get-tuple-element.386, bf16[8,1,8,4096]{3,2,1,0:T(8,128)(2,1)S(1)} %get-tuple-element.388, s32[]{:T(128)} %get-tuple-element.371, bf16[8,1,8,512]{3,2,1,0:T(8,128)(2,1)S(1)} %get-tuple-element.387), kind=kOutput, calls=%fused_computation.9.clone.1 | convolution fusion | flops 1115684864 | bytes 648192 | tf_op jit(solution)/shard_map/while/body/eval_jaxpr/bpk,ks->bps/dot_general | solution.py:66
  25.8 3.3 %fusion.88 = f32[1,512,256]{2,1,0:T(8,128)S(1)} fusion(s32[4096]{0:T(1024)} %get-tuple-element.392, f32[4096]{0:T(1024)} %get-tuple-element.389, f32[4096]{0:T(1024)} %get-tuple-element.386, bf16[8,1,8,4096]{3,2,1,0:T(8,128)(2,1)S(1)} %get-tuple-element.388, s32[]{:T(128)} %get-tuple-element.371, bf16[8,1,8,512]{3,2,1,0:T(8,128)(2,1)S(1)} %get-tuple-element.387), kind=kOutput, calls=%fused_computation.9.clone.1 | convolution fusion | flops 1115684864 | bytes 648192 | tf_op jit(solution)/shard_map/while/body/eval_jaxpr/bpk,ks->bps/dot_general | solution.py:66
  32.1 3.3 %fusion.88 = f32[1,512,256]{2,1,0:T(8,128)S(1)} fusion(s32[4096]{0:T(1024)} %get-tuple-element.392, f32[4096]{0:T(1024)} %get-tuple-element.389, f32[4096]{0:T(1024)} %get-tuple-element.386, bf16[8,1,8,4096]{3,2,1,0:T(8,128)(2,1)S(1)} %get-tuple-element.388, s32[]{:T(128)} %get-tuple-element.371, bf16[8,1,8,512]{3,2,1,0:T(8,128)(2,1)S(1)} %get-tuple-element.387), kind=kOutput, calls=%fused_computation.9.clone.1 | convolution fusion | flops 1115684864 | bytes 648192 | tf_op jit(solution)/shard_map/while/body/eval_jaxpr/bpk,ks->bps/dot_general | solution.py:66
  37.3 1.1 fusion.89
  38.5 3.3 %fusion.88 = f32[1,512,256]{2,1,0:T(8,128)S(1)} fusion(s32[4096]{0:T(1024)} %get-tuple-element.392, f32[4096]{0:T(1024)} %get-tuple-element.389, f32[4096]{0:T(1024)} %get-tuple-element.386, bf16[8,1,8,4096]{3,2,1,0:T(8,128)(2,1)S(1)} %get-tuple-element.388, s32[]{:T(128)} %get-tuple-element.371, bf16[8,1,8,512]{3,2,1,0:T(8,128)(2,1)S(1)} %get-tuple-element.387), kind=kOutput, calls=%fused_computation.9.clone.1 | convolution fusion | flops 1115684864 | bytes 648192 | tf_op jit(solution)/shard_map/while/body/eval_jaxpr/bpk,ks->bps/dot_general | solution.py:66
  43.7 1.2 fusion.89
  44.8 3.3 %fusion.88 = f32[1,512,256]{2,1,0:T(8,128)S(1)} fusion(s32[4096]{0:T(1024)} %get-tuple-element.392, f32[4096]{0:T(1024)} %get-tuple-element.389, f32[4096]{0:T(1024)} %get-tuple-element.386, bf16[8,1,8,4096]{3,2,1,0:T(8,128)(2,1)S(1)} %get-tuple-element.388, s32[]{:T(128)} %get-tuple-element.371, bf16[8,1,8,512]{3,2,1,0:T(8,128)(2,1)S(1)} %get-tuple-element.387), kind=kOutput, calls=%fused_computation.9.clone.1 | convolution fusion | flops 1115684864 | bytes 648192 | tf_op jit(solution)/shard_map/while/body/eval_jaxpr/bpk,ks->bps/dot_general | solution.py:66
  50.0 1.2 fusion.89
  51.2 3.3 %fusion.88 = f32[1,512,256]{2,1,0:T(8,128)S(1)} fusion(s32[4096]{0:T(1024)} %get-tuple-element.392, f32[4096]{0:T(1024)} %get-tuple-element.389, f32[4096]{0:T(1024)} %get-tuple-element.386, bf16[8,1,8,4096]{3,2,1,0:T(8,128)(2,1)S(1)} %get-tuple-element.388, s32[]{:T(128)} %get-tuple-element.371, bf16[8,1,8,512]{3,2,1,0:T(8,128)(2,1)S(1)} %get-tuple-element.387), kind=kOutput, calls=%fused_computation.9.clone.1 | convolution fusion | flops 1115684864 | bytes 648192 | tf_op jit(solution)/shard_map/while/body/eval_jaxpr/bpk,ks->bps/dot_general | solution.py:66
  57.5 3.3 %fusion.88 = f32[1,512,256]{2,1,0:T(8,128)S(1)} fusion(s32[4096]{0:T(1024)} %get-tuple-element.392, f32[4096]{0:T(1024)} %get-tuple-element.389, f32[4096]{0:T(1024)} %get-tuple-element.386, bf16[8,1,8,4096]{3,2,1,0:T(8,128)(2,1)S(1)} %get-tuple-element.388, s32[]{:T(128)} %get-tuple-element.371, bf16[8,1,8,512]{3,2,1,0:T(8,128)(2,1)S(1)} %get-tuple-element.387), kind=kOutput, calls=%fused_computation.9.clone.1 | convolution fusion | flops 1115684864 | bytes 648192 | tf_op jit(solution)/shard_map/while/body/eval_jaxpr/bpk,ks->bps/dot_general | solution.py:66
  63.8 3.3 %fusion.88 = f32[1,512,256]{2,1,0:T(8,128)S(1)} fusion(s32[4096]{0:T(1024)} %get-tuple-element.392, f32[4096]{0:T(1024)} %get-tuple-element.389, f32[4096]{0:T(1024)} %get-tuple-element.386, bf16[8,1,8,4096]{3,2,1,0:T(8,128)(2,1)S(1)} %get-tuple-element.388, s32[]{:T(128)} %get-tuple-element.371, bf16[8,1,8,512]{3,2,1,0:T(8,128)(2,1)S(1)} %get-tuple-element.387), kind=kOutput, calls=%fused_computation.9.clone.1 | convolution fusion | flops 1115684864 | bytes 648192 | tf_op jit(solution)/shard_map/while/body/eval_jaxpr/bpk,ks->bps/dot_general | solution.py:66
  69.0 1.2 fusion.89
  70.2 4.4 %collective-permute-done = f32[8,512,128]{2,1,0:T(8,128)S(1)} collective-permute-done((f32[8,512,128]{2,1,0:T(8,128)}, f32[8,512,128]{2,1,0:T(8,128)S(1)}, u32[]{:S(2)}, u32[]{:S(2)}) %collective-permute-start) | collective-permute-done | bytes 2097184 | tf_op jit(solution)/shard_map/ppermute | solution.py:14
  74.6 1.9 bitcast_add_fusion
  76.5 1.6 collective-permute-start.1
  78.0 46.2 %collective-permute-done.1 = f32[8,512,128]{2,1,0:T(8,128)S(1)} collective-permute-done((f32[8,512,128]{2,1,0:T(8,128)S(1)}, f32[8,512,128]{2,1,0:T(8,128)S(1)}, u32[]{:S(2)}, u32[]{:S(2)}) %collective-permute-start.1) | collective-permute-done | bytes 2097184 | tf_op jit(solution)/shard_map/ppermute | solution.py:14
  124.2 1.5 add.29
  125.8 1.5 collective-permute-start.2
  127.4 45.5 %collective-permute-done.2 = f32[8,512,128]{2,1,0:T(8,128)} collective-permute-done((f32[8,512,128]{2,1,0:T(8,128)}, f32[8,512,128]{2,1,0:T(8,128)}, u32[]{:S(2)}, u32[]{:S(2)}) %collective-permute-start.2) | collective-permute-done | bytes 2097184 | tf_op jit(solution)/shard_map/ppermute | solution.py:14
  172.9 2.8 fusion.62
  175.7 88.5 %while.27 = (s32[]{:T(128)}, f32[8,1,8,4096]{3,2,1,0:T(8,128)}, f32[8,1,8,512]{3,2,1,0:T(8,128)}, bf16[8,1,8,512]{3,2,1,0:T(8,128)(2,1)S(1)}, bf16[8,1,512,128]{...) while((s32[]{:T(128)}, f32[8,1,8,4096]{3,2,1,0:T(8,128)}, ...), condition=%wide.region_3.4_spmd.clone, body=%wide.region_2.3_spmd.clone.sunk | while | flops 1200193536 | bytes 31266512 | solution.py:110
  177.6 2.6 fusion.100
  180.2 2.5 multiply_convert_fusion.4
  182.8 1.3 fusion.101
  184.1 2.6 fusion.102
  188.6 2.6 fusion.100
  191.3 2.5 multiply_convert_fusion.4
  193.8 1.3 fusion.101
  195.2 2.6 fusion.102
  199.7 2.6 fusion.100
  202.3 2.5 multiply_convert_fusion.4
  204.9 1.3 fusion.101
  206.2 2.6 fusion.102
  210.8 2.6 fusion.100
  213.4 2.5 multiply_convert_fusion.4
  216.0 1.3 fusion.101
  217.3 2.7 fusion.102
  221.8 2.6 fusion.100
  224.5 2.5 multiply_convert_fusion.4
  227.0 1.3 fusion.101
  228.4 2.6 fusion.102
  232.9 2.6 fusion.100
  235.5 2.5 multiply_convert_fusion.4
  238.1 1.3 fusion.101
  239.4 2.6 fusion.102
  244.0 2.6 fusion.100
  246.6 2.5 multiply_convert_fusion.4
  249.2 1.3 fusion.101
  250.5 2.6 fusion.102
  255.0 2.6 fusion.100
  257.7 2.5 multiply_convert_fusion.4
  260.2 1.3 fusion.101
  261.5 2.6 fusion.102
  264.2 2.9 copy.18
  267.0 3.1 bitcast_bitcast_fusion
  270.1 2.7 reshape.144
  272.8 8.3 %all_to_all.33 = f32[4,1,8192]{2,1,0:T(1,128)S(1)} all-to-all(f32[4,1,8192]{2,1,0:T(1,128)S(1)} %reshape.144), channel_id=1, replica_groups=mesh['path'=4,'trade'=8] {'path'}, dimensions={0} | all-to-all | bytes 262144 | tf_op jit(solution)/shard_map/all_to_all | solution.py:116
  282.6 2.5 reshape.145
  285.1 2.8 copy.19
  287.9 2.3 fusion.61
  290.2 30.5 %reduce-scatter.2.cloned.1.call-done = f32[4,8,128]{2,1,0:T(8,128)} async-done(((f32[32,8,128]{2,1,0:T(8,128)}), f32[4,8,128]{2,1,0:T(8,128)}) %reduce-scatter.2.cloned.1.call-update) | async-done | bytes 16400 | tf_op jit(solution)/shard_map/reduce_scatter | solution.py:117
  (158 shorter events, 37.1 us)
Async XLA Ops:
  7.2 6.5 %copy-start = (bf16[32,8,4096]{2,1,0:T(8,128)(2,1)S(1)}, bf16[32,8,4096]{2,1,0:T(8,128)(2,1)}, u32[]{:S(2)}) copy-start(bf16[32,8,4096]{2,1,0:T(8,128)(2,1)} %param.14) | copy-start | bytes 6291460
  7.2 12.2 %all-to-all-start = ((bf16[32,8,128]{2,1,0:T(8,128)(2,1)}), bf16[32,8,128]{2,1,0:T(8,128)(2,1)S(1)}, u32[]{:S(2)}, u32[]{:S(2)}) async-start(bf16[32,8,128]{2,1,0:T(8,128)(2,1)} %param.13), calls=%async_computation | async-start | bytes 131072 | tf_op jit(solution)/shard_map/all_to_all | solution.py:38
  13.7 307.0 %reduce-scatter.2.cloned.1.call-start = ((), (), s32[]{:S(2)}) async-start(), calls=%async_computation.3 | async-start | bytes 147456 | tf_op jit(solution)/shard_map/reduce_scatter | solution.py:117
  19.4 3.9 %copy-start.9 = (f32[128]{0:T(128)S(1)}, f32[128]{0:T(128)}, u32[]{:S(2)}) copy-start(f32[128]{0:T(128)} %get-tuple-element.391) | copy-start | bytes 1540 | tf_op jit(solution)/shard_map/while
  19.5 5.2 %copy-start.5 = (s32[128]{0:T(128)S(1)}, s32[128]{0:T(128)}, u32[]{:S(2)}) copy-start(s32[128]{0:T(128)} %get-tuple-element.393) | copy-start | bytes 1540 | tf_op jit(solution)/shard_map/while
  25.8 3.9 %copy-start.9 = (f32[128]{0:T(128)S(1)}, f32[128]{0:T(128)}, u32[]{:S(2)}) copy-start(f32[128]{0:T(128)} %get-tuple-element.391) | copy-start | bytes 1540 | tf_op jit(solution)/shard_map/while
  25.8 5.2 %copy-start.5 = (s32[128]{0:T(128)S(1)}, s32[128]{0:T(128)}, u32[]{:S(2)}) copy-start(s32[128]{0:T(128)} %get-tuple-element.393) | copy-start | bytes 1540 | tf_op jit(solution)/shard_map/while
  32.1 3.9 %copy-start.9 = (f32[128]{0:T(128)S(1)}, f32[128]{0:T(128)}, u32[]{:S(2)}) copy-start(f32[128]{0:T(128)} %get-tuple-element.391) | copy-start | bytes 1540 | tf_op jit(solution)/shard_map/while
  32.1 5.2 %copy-start.5 = (s32[128]{0:T(128)S(1)}, s32[128]{0:T(128)}, u32[]{:S(2)}) copy-start(s32[128]{0:T(128)} %get-tuple-element.393) | copy-start | bytes 1540 | tf_op jit(solution)/shard_map/while
  38.5 3.9 %copy-start.9 = (f32[128]{0:T(128)S(1)}, f32[128]{0:T(128)}, u32[]{:S(2)}) copy-start(f32[128]{0:T(128)} %get-tuple-element.391) | copy-start | bytes 1540 | tf_op jit(solution)/shard_map/while
  38.5 5.2 %copy-start.5 = (s32[128]{0:T(128)S(1)}, s32[128]{0:T(128)}, u32[]{:S(2)}) copy-start(s32[128]{0:T(128)} %get-tuple-element.393) | copy-start | bytes 1540 | tf_op jit(solution)/shard_map/while
  44.8 3.9 %copy-start.9 = (f32[128]{0:T(128)S(1)}, f32[128]{0:T(128)}, u32[]{:S(2)}) copy-start(f32[128]{0:T(128)} %get-tuple-element.391) | copy-start | bytes 1540 | tf_op jit(solution)/shard_map/while
  44.8 5.2 %copy-start.5 = (s32[128]{0:T(128)S(1)}, s32[128]{0:T(128)}, u32[]{:S(2)}) copy-start(s32[128]{0:T(128)} %get-tuple-element.393) | copy-start | bytes 1540 | tf_op jit(solution)/shard_map/while
  51.2 3.9 %copy-start.9 = (f32[128]{0:T(128)S(1)}, f32[128]{0:T(128)}, u32[]{:S(2)}) copy-start(f32[128]{0:T(128)} %get-tuple-element.391) | copy-start | bytes 1540 | tf_op jit(solution)/shard_map/while
  51.2 5.2 %copy-start.5 = (s32[128]{0:T(128)S(1)}, s32[128]{0:T(128)}, u32[]{:S(2)}) copy-start(s32[128]{0:T(128)} %get-tuple-element.393) | copy-start | bytes 1540 | tf_op jit(solution)/shard_map/while
  57.5 3.9 %copy-start.9 = (f32[128]{0:T(128)S(1)}, f32[128]{0:T(128)}, u32[]{:S(2)}) copy-start(f32[128]{0:T(128)} %get-tuple-element.391) | copy-start | bytes 1540 | tf_op jit(solution)/shard_map/while
  57.5 5.2 %copy-start.5 = (s32[128]{0:T(128)S(1)}, s32[128]{0:T(128)}, u32[]{:S(2)}) copy-start(s32[128]{0:T(128)} %get-tuple-element.393) | copy-start | bytes 1540 | tf_op jit(solution)/shard_map/while
  63.8 3.9 %copy-start.9 = (f32[128]{0:T(128)S(1)}, f32[128]{0:T(128)}, u32[]{:S(2)}) copy-start(f32[128]{0:T(128)} %get-tuple-element.391) | copy-start | bytes 1540 | tf_op jit(solution)/shard_map/while
  63.8 5.2 %copy-start.5 = (s32[128]{0:T(128)S(1)}, s32[128]{0:T(128)}, u32[]{:S(2)}) copy-start(s32[128]{0:T(128)} %get-tuple-element.393) | copy-start | bytes 1540 | tf_op jit(solution)/shard_map/while
  70.2 6.2 %copy-start.1 = (bf16[8,1,8,4096]{3,2,1,0:T(8,128)(2,1)}, bf16[8,1,8,4096]{3,2,1,0:T(8,128)(2,1)S(1)}, u32[]{:S(2)}) copy-start(bf16[8,1,8,4096]{3,2,1,0:T(8,128)(2,1)S(1)} %get-tuple-element.430) | copy-start | bytes 1572868
  70.2 4.4 %collective-permute-start = (f32[8,512,128]{2,1,0:T(8,128)}, f32[8,512,128]{2,1,0:T(8,128)S(1)}, u32[]{:S(2)}, u32[]{:S(2)}) collective-permute-start(f32[8,512,128]{2,1,0:T(8,128)} %bitcast.118), channel_id=1, source_target_pairs={{0,1},{1,0},{2,3},{3,2},{4,5},{5,4},{6,7},{7,6},{8,9},{9,8},{10,11... | collective-permute-start | bytes 6291464 | tf_op jit(solution)/shard_map/ppermute | solution.py:14
  76.4 50.8 %copy-start.10 = (f32[32]{0:T(128)S(1)}, f32[32]{0:T(128)}, u32[]{:S(2)}) copy-start(f32[32]{0:T(128)} %param.17) | copy-start | bytes 388
  76.5 50.9 %copy-start.8 = (f32[128]{0:T(128)S(1)}, f32[128]{0:T(128)}, u32[]{:S(2)}) copy-start(f32[128]{0:T(128)} %param.18) | copy-start | bytes 1540
  76.5 47.7 %collective-permute-start.1 = (f32[8,512,128]{2,1,0:T(8,128)S(1)}, f32[8,512,128]{2,1,0:T(8,128)S(1)}, u32[]{:S(2)}, u32[]{:S(2)}) collective-permute-start(f32[8,512,128]{2,1,0:T(8,128)S(1)} %bitcast_add_fusion), channel_id=1, source_target_pairs={{0,2},{1,3},{2,0},{3,1},{4,6},{5,7},{6,4},{7,5},{8,10},{9,11},{10,... | collective-permute-start | bytes 6291464 | tf_op jit(solution)/shard_map/ppermute | solution.py:14
  125.8 47.1 %collective-permute-start.2 = (f32[8,512,128]{2,1,0:T(8,128)}, f32[8,512,128]{2,1,0:T(8,128)}, u32[]{:S(2)}, u32[]{:S(2)}) collective-permute-start(f32[8,512,128]{2,1,0:T(8,128)} %add.29), channel_id=1, source_target_pairs={{0,4},{1,5},{2,6},{3,7},{4,0},{5,1},{6,2},{7,3},{8,12},{9,13},{10,... | collective-permute-start | bytes 6291464 | tf_op jit(solution)/shard_map/ppermute | solution.py:14
  127.4 48.2 %copy-start.2 = (f32[4096]{0:T(1024)S(1)}, f32[4096]{0:T(1024)}, u32[]{:S(2)}) copy-start(f32[4096]{0:T(1024)} %get-tuple-element.436) | copy-start | bytes 49156
  127.4 48.3 %copy-start.6 = (s32[128]{0:T(128)S(1)}, s32[128]{0:T(128)}, u32[]{:S(2)}) copy-start(s32[128]{0:T(128)} %get-tuple-element.442) | copy-start | bytes 1540
  175.7 0.6 copy-start.3
  180.2 2.6 copy-start.4
  184.1 2.6 copy-start.7
  186.8 0.6 copy-start.3
  191.3 2.6 copy-start.4
  195.2 2.6 copy-start.7
  197.8 0.6 copy-start.3
  202.3 2.6 copy-start.4
  206.2 2.7 copy-start.7
  208.9 0.6 copy-start.3
  213.4 2.6 copy-start.4
  217.3 2.7 copy-start.7
  219.9 0.6 copy-start.3
  224.5 2.6 copy-start.4
  228.4 2.7 copy-start.7
  231.0 0.6 copy-start.3
  235.5 2.6 copy-start.4
  239.4 2.6 copy-start.7
  242.1 0.6 copy-start.3
  246.6 2.6 copy-start.4
  250.5 2.6 copy-start.7
  253.1 0.6 copy-start.3
  257.6 2.6 copy-start.4
  261.5 2.6 copy-start.7
Sparse Core Ops, SparseCore 0:
  288.0 32.6 reduce-scatter.1
